TPU v7x, 32 devices: a whole 2x2x4 slice. The times are simulated.
32 devices in a mesh: member: 8 (over z, core), dp: 4 (over y, x).
Axes of the slice: x: 2, y: 2, z: 4, core: 2. Of those that a mesh axis runs over, the one named last changes fastest.
Arguments:
- feats: bfloat16 [8, 2048, 1024], P('member', 'dp'), may hold values from -160 to 160
- pair_weight: float32 [8, 3], replicated, may hold values from 0.5 to 2
Outputs:
- grad_centred: float32 [8, 2048, 1024], P('member', 'dp')
- cka: float32 [8, 3], P('member')
All inputs are finite; a program needn't handle non-finite values.
Results may differ from a plain program's by a relative error of at most 0.0053.
Values may be sent and summed in bfloat16 or wider, within the bound.
A program may use at most 128 MiB of HBM per device.

v0:
```python
import math
import jax
import jax.numpy as jnp
from jax import lax
from jax.sharding import PartitionSpec as P


def mixing(self_hsic, pair_hsic, pair_weight):
    pairs = pair_weight.shape[1]
    members = pair_weight.shape[0]
    partner_self = jnp.stack([jnp.roll(self_hsic, -o) for o in range(1, pairs + 1)], axis=1)
    norms = jnp.sqrt(self_hsic[:, None] * partner_self)
    cka = pair_hsic / norms
    weighted = pair_weight * cka
    incoming = sum((jnp.roll(weighted[:, o - 1], o) for o in range(1, pairs + 1)))
    self_coef = (jnp.sum(weighted, axis=1) + incoming) / (self_hsic + 1e-06)
    coef = 2.0 * pair_weight / norms
    eye = jnp.eye(members, dtype=jnp.float32)
    mix = -2.0 * self_coef[:, None] * eye
    for o in range(1, pairs + 1):
        ahead = coef[:, o - 1][:, None] * jnp.roll(eye, o, axis=1)
        mix = mix + ahead + ahead.T
    return (cka, mix)


def shards(feats, pair_weight):
    rows = feats[0]
    members = lax.axis_size("member")
    pairs = pair_weight.shape[1]
    whole = lax.all_gather(rows, "dp", axis=0, tiled=True)
    batch, width = whole.shape
    mean = jnp.sum(whole.astype(jnp.float32), axis=0) / batch
    centred = (whole.astype(jnp.float32) - mean).astype(jnp.bfloat16)
    own = (rows.astype(jnp.float32) - mean).astype(jnp.bfloat16)
    blocks = centred.reshape(members, batch // members, width)
    gram = jnp.einsum("rf,mcf->mrc", own, blocks, preferred_element_type=jnp.float32)
    held = lax.all_to_all(gram.astype(jnp.bfloat16), "member", 0, 0)
    held = held.astype(jnp.float32)
    sums = []
    for o in range(pairs + 1):
        sums.append(jnp.sum(held * jnp.roll(held, -o, axis=0), axis=(1, 2)))
    sums = lax.psum(jnp.stack(sums, axis=1), ("member", "dp"))
    cka, mix = mixing(sums[:, 0], sums[:, 1:], pair_weight)
    mixed = jnp.stack(
        [sum((mix[m, q] * held[q] for q in range(members))) for m in range(members)]
    ).astype(jnp.bfloat16)
    mixed = lax.all_to_all(mixed, "member", 0, 0)
    grad = jnp.einsum("jrc,jcf->rf", mixed, blocks, preferred_element_type=jnp.float32)
    grad = math.sqrt(batch) * grad
    own_cka = lax.dynamic_slice_in_dim(cka, lax.axis_index("member"), 1, axis=0)
    return (grad[None], own_cka)


def solution(mesh):
    return jax.shard_map(
        shards,
        mesh=mesh,
        in_specs=(P("member", "dp", None), P()),
        out_specs=(P("member", "dp", None), P("member", None)),
        check_vma=False,
    )
```

profile of v0, /device:TPU:0, one launch (start us, length us, event | category | flops | bytes accessed | tf_op | source)
XLA Modules:
  0.0 292.4 jit_solution(5384150362921916437)
XLA Ops:
  7.2 0.0 all-gather.3.cloned.1.call-start
  7.2 0.7 all-gather.3.cloned.1.call-update
  7.9 57.2 %all-gather.3.cloned.1.call-done = bf16[1,2048,1024]{2,1,0:T(8,128)(2,1)} async-done(((bf16[1,512,1024]{2,1,0:T(8,128)(2,1)}), bf16[1,2048,1024]{2,1,0:T(8,128)(2,1)}) %all-gather.3.cloned.1.call-update) | async-done | bytes 4194320 | tf_op jit(solution)/shard_map/all_gather | solution.py:30
  65.1 0.0 copy-start.1
  65.1 3.0 %convert_reduce_fusion = f32[1024]{0:T(1024)S(1)} fusion(bf16[1,2048,1024]{2,1,0:T(8,128)(2,1)} %all-gather.3.cloned.1.call-done), kind=kLoop, calls=%fused_computation | loop fusion | flops 4193280 | bytes 4198400 | tf_op jit(solution)/shard_map/reduce_sum | solution.py:32
  68.2 0.4 copy-done.1
  68.6 1.3 fusion.1
  69.9 0.0 copy-start
  69.9 1.9 copy-done
  71.8 0.0 copy-done.2
  71.8 3.8 %convert_bitcast_fusion.1 = bf16[8,512,256]{1,2,0:T(8,128)(2,1)} fusion(bf16[8,256,1024]{2,1,0:T(8,128)(2,1)S(1)} %bitcast.136, bf16[1,512,1024]{2,1,0:T(8,128)(2,1)S(1)} %copy-done.2, f32[1024]{0:T(1024)S(1)} %broadcast_multiply_fusion), kind=kOutput, calls=%fused_computation.13 | convolution fusion | flops 2150105088 | bytes 7344128 | tf_op jit(solution)/shard_map/rf,mcf->mrc/dot_general | solution.py:36
  75.5 4.6 %all-to-all-start = ((bf16[8,512,256]{1,2,0:T(8,128)(2,1)}), bf16[8,512,256]{1,2,0:T(8,128)(2,1)S(1)}, u32[]{:S(2)}, u32[]{:S(2)}) async-start(bf16[8,512,256]{1,2,0:T(8,128)(2,1)} %convert_bitcast_fusion.1), calls=%async_computation | async-start | bytes 4194304 | tf_op jit(solution)/shard_map/all_to_all | solution.py:37
  80.1 0.1 slice.447
  80.2 0.1 slice.450
  80.3 0.1 slice.453
  80.4 0.1 copy.13
  80.4 0.1 copy.14
  80.5 48.6 %all-to-all-done = bf16[8,512,256]{1,2,0:T(8,128)(2,1)S(1)} async-done(((bf16[8,512,256]{1,2,0:T(8,128)(2,1)}), bf16[8,512,256]{1,2,0:T(8,128)(2,1)S(1)}, u32[]{:S(2)}, u32[]{:S(2)}) %all-to-all-start) | async-done | bytes 2097184 | tf_op jit(solution)/shard_map/all_to_all | solution.py:37
  129.2 0.5 slice.526
  129.7 0.4 slice.528
  130.1 0.4 slice.530
  130.5 0.2 slice.531
  130.7 0.1 slice.529
  130.8 0.1 slice.527
  130.9 0.0 copy-start.3
  130.9 1.8 multiply_reduce_fusion
  132.7 0.1 copy.4
  132.8 37.0 %psum.7 = f32[8,4]{0,1:T(4,128)S(1)} all-reduce(f32[8,4]{0,1:T(4,128)S(1)} %pad_maximum_fusion), channel_id=1, replica_groups=mesh['member'=8,'dp'=4] {'member','dp'}, use_global_device_ids=true, to_apply=%region_5.6 | all-reduce | flops 32 | bytes 256 | tf_op jit(solution)/shard_map/psum | solution.py:42
  169.8 0.5 slice.430
  170.3 0.1 slice_bitcast_fusion.7
  170.4 0.1 slice_bitcast_fusion.6
  170.4 0.1 slice_bitcast_fusion.4
  170.5 0.7 maximum_bitcast_fusion
  171.2 0.1 maximum_bitcast_fusion.1
  171.3 0.1 maximum_bitcast_fusion.2
  171.4 0.0 copy-done.3
  171.4 0.6 slice.440
  172.0 0.1 slice.442
  172.1 0.1 slice.444
  172.2 0.7 slice_bitcast_fusion.1
  172.9 0.1 copy.7
  173.0 0.1 fusion.18
  173.0 0.1 copy.8
  173.1 0.1 maximum_multiply_fusion.5
  173.2 0.1 copy.9
  173.3 0.1 bitcast_add_fusion
  173.3 0.7 fusion.26
  174.1 0.6 fusion.27
  174.7 0.7 fusion.25
  175.4 0.7 fusion.24
  176.1 0.6 convert_element_type.47
  176.7 6.4 %fusion.9 = bf16[8,512,256]{1,2,0:T(8,128)(2,1)} fusion(f32[8,512,256]{1,2,0:T(8,128)S(1)} %convert_element_type.47, f32[]{:T(128)} %bitcast.34, f32[]{:T(128)} %bitcast.33, f32[]{:T(128)} %bitcast.32, f32[]{:T(128)} %bitcast.31, f32[]{:T(128)} %bitcast.30, f32[]{:T(128)} %bitcast.29, f32[]{:T(128)} %bitcast.28, f32[]{:T(128)} %bitcast.27), kind=kLoop, calls=%fused_computation.25 | loop fusion | flops 2097151 | bytes 4456480
  183.1 6.1 %fusion.10 = bf16[8,512,256]{1,2,0:T(8,128)(2,1)} fusion(bf16[8,512,256]{1,2,0:T(8,128)(2,1)} %fusion.9, f32[8,512,256]{1,2,0:T(8,128)S(1)} %convert_element_type.47, f32[]{:T(128)} %bitcast.42, f32[]{:T(128)} %bitcast.41, f32[]{:T(128)} %bitcast.40, f32[]{:T(128)} %bitcast.39, f32[]{:T(128)} %bitcast.38, f32[]{:T(128)} %bitcast.37, f32[]{:T(128)} %bitcast.36, ...), kind=kLoop, calls=%fused_computation.26 | loop fusion | flops 2097152 | bytes 4460544
  189.2 6.1 %fusion.11 = bf16[8,512,256]{1,2,0:T(8,128)(2,1)} fusion(bf16[8,512,256]{1,2,0:T(8,128)(2,1)} %fusion.10, f32[8,512,256]{1,2,0:T(8,128)S(1)} %convert_element_type.47, f32[]{:T(128)} %bitcast.50, f32[]{:T(128)} %bitcast.49, f32[]{:T(128)} %bitcast.48, f32[]{:T(128)} %bitcast.47, f32[]{:T(128)} %bitcast.46, f32[]{:T(128)} %bitcast.45, f32[]{:T(128)} %bitcast.44, ...), kind=kLoop, calls=%fused_computation.27 | loop fusion | flops 2097152 | bytes 4460544
  195.3 6.1 %fusion.12 = bf16[8,512,256]{1,2,0:T(8,128)(2,1)} fusion(bf16[8,512,256]{1,2,0:T(8,128)(2,1)} %fusion.11, f32[8,512,256]{1,2,0:T(8,128)S(1)} %convert_element_type.47, f32[]{:T(128)} %bitcast.58, f32[]{:T(128)} %bitcast.57, f32[]{:T(128)} %bitcast.56, f32[]{:T(128)} %bitcast.55, f32[]{:T(128)} %bitcast.54, f32[]{:T(128)} %bitcast.53, f32[]{:T(128)} %bitcast.52, ...), kind=kLoop, calls=%fused_computation.28 | loop fusion | flops 2097152 | bytes 4460544
  201.4 6.3 %fusion.13 = bf16[8,512,256]{1,2,0:T(8,128)(2,1)} fusion(bf16[8,512,256]{1,2,0:T(8,128)(2,1)} %fusion.12, f32[8,512,256]{1,2,0:T(8,128)S(1)} %convert_element_type.47, f32[]{:T(128)} %bitcast.66, f32[]{:T(128)} %bitcast.65, f32[]{:T(128)} %bitcast.64, f32[]{:T(128)} %bitcast.63, f32[]{:T(128)} %bitcast.62, f32[]{:T(128)} %bitcast.61, f32[]{:T(128)} %bitcast.60, ...), kind=kLoop, calls=%fused_computation.29 | loop fusion | flops 2097152 | bytes 4460544
  207.7 6.2 %fusion.14 = bf16[8,512,256]{1,2,0:T(8,128)(2,1)} fusion(bf16[8,512,256]{1,2,0:T(8,128)(2,1)} %fusion.13, f32[8,512,256]{1,2,0:T(8,128)S(1)} %convert_element_type.47, f32[]{:T(128)} %bitcast.74, f32[]{:T(128)} %bitcast.73, f32[]{:T(128)} %bitcast.72, f32[]{:T(128)} %bitcast.71, f32[]{:T(128)} %bitcast.70, f32[]{:T(128)} %bitcast.69, f32[]{:T(128)} %bitcast.68, ...), kind=kLoop, calls=%fused_computation.30 | loop fusion | flops 2097152 | bytes 4460544
  214.0 6.2 %fusion.15 = bf16[8,512,256]{1,2,0:T(8,128)(2,1)} fusion(bf16[8,512,256]{1,2,0:T(8,128)(2,1)} %fusion.14, f32[8,512,256]{1,2,0:T(8,128)S(1)} %convert_element_type.47, f32[]{:T(128)} %bitcast.82, f32[]{:T(128)} %bitcast.81, f32[]{:T(128)} %bitcast.80, f32[]{:T(128)} %bitcast.79, f32[]{:T(128)} %bitcast.78, f32[]{:T(128)} %bitcast.77, f32[]{:T(128)} %bitcast.76, ...), kind=kLoop, calls=%fused_computation.31 | loop fusion | flops 2097152 | bytes 4460544
  220.2 6.2 %fusion.16 = bf16[8,512,256]{1,2,0:T(8,128)(2,1)} fusion(bf16[8,512,256]{1,2,0:T(8,128)(2,1)} %fusion.15, f32[8,512,256]{1,2,0:T(8,128)S(1)} %convert_element_type.47, f32[]{:T(128)} %bitcast.90, f32[]{:T(128)} %bitcast.89, f32[]{:T(128)} %bitcast.88, f32[]{:T(128)} %bitcast.87, f32[]{:T(128)} %bitcast.86, f32[]{:T(128)} %bitcast.85, f32[]{:T(128)} %bitcast.84, ...), kind=kLoop, calls=%fused_computation.32 | loop fusion | flops 2097152 | bytes 4460544 | tf_op jit(solution)/shard_map/stack | solution.py:44
  226.4 4.2 %all-to-all-start.1 = ((bf16[8,512,256]{1,2,0:T(8,128)(2,1)}), bf16[8,512,256]{1,2,0:T(8,128)(2,1)S(1)}, u32[]{:S(2)}, u32[]{:S(2)}) async-start(bf16[8,512,256]{1,2,0:T(8,128)(2,1)} %fusion.16), calls=%async_computation.1 | async-start | bytes 4194304 | tf_op jit(solution)/shard_map/all_to_all | solution.py:47
  230.6 0.1 constant_dynamic-slice_fusion
  230.7 0.6 copy.11
  231.3 48.4 %all-to-all-done.1 = bf16[8,512,256]{1,2,0:T(8,128)(2,1)S(1)} async-done(((bf16[8,512,256]{1,2,0:T(8,128)(2,1)}), bf16[8,512,256]{1,2,0:T(8,128)(2,1)S(1)}, u32[]{:S(2)}, u32[]{:S(2)}) %all-to-all-start.1) | async-done | bytes 2097184 | tf_op jit(solution)/shard_map/all_to_all | solution.py:47
  279.7 5.9 %fusion.5 = f32[1,512,1024]{2,1,0:T(8,128)} fusion(bf16[8,512,256]{1,2,0:T(8,128)(2,1)S(1)} %all-to-all-done.1, bf16[8,256,1024]{2,1,0:T(8,128)(2,1)} %bitcast.137), kind=kOutput, calls=%fused_computation.12 | convolution fusion | flops 2148007936 | bytes 8388608 | tf_op jit(solution)/shard_map/jrc,jcf->rf/dot_general | solution.py:48
  (13 shorter events, 0.1 us)
Async XLA Ops:
  7.2 58.0 %all-gather.3.cloned.1.call-start = ((), (), s32[]{:S(2)}) async-start(), calls=%async_computation.2 | async-start | bytes 5242880 | tf_op jit(solution)/shard_map/all_gather | solution.py:30
  65.1 3.4 %copy-start.1 = (bf16[1,2048,1024]{2,1,0:T(8,128)(2,1)S(1)}, bf16[1,2048,1024]{2,1,0:T(8,128)(2,1)}, u32[]{:S(2)}) copy-start(bf16[1,2048,1024]{2,1,0:T(8,128)(2,1)} %all-gather.3.cloned.1.call-done) | copy-start | bytes 12582916
  68.6 3.2 %copy-start.2 = (bf16[1,512,1024]{2,1,0:T(8,128)(2,1)S(1)}, bf16[1,512,1024]{2,1,0:T(8,128)(2,1)}, u32[]{:S(2)}) copy-start(bf16[1,512,1024]{2,1,0:T(8,128)(2,1)} %param.2) | copy-start | bytes 3145732
  69.9 1.9 copy-start
  75.5 53.6 %all-to-all-start = ((bf16[8,512,256]{1,2,0:T(8,128)(2,1)}), bf16[8,512,256]{1,2,0:T(8,128)(2,1)S(1)}, u32[]{:S(2)}, u32[]{:S(2)}) async-start(bf16[8,512,256]{1,2,0:T(8,128)(2,1)} %convert_bitcast_fusion.1), calls=%async_computation | async-start | bytes 4194304 | tf_op jit(solution)/shard_map/all_to_all | solution.py:37
  130.9 40.5 %copy-start.3 = (f32[8,3]{0,1:T(4,128)S(1)}, f32[8,3]{0,1:T(4,128)}, u32[]{:S(2)}) copy-start(f32[8,3]{0,1:T(4,128)} %param.3) | copy-start | bytes 292
  226.4 53.3 %all-to-all-start.1 = ((bf16[8,512,256]{1,2,0:T(8,128)(2,1)}), bf16[8,512,256]{1,2,0:T(8,128)(2,1)S(1)}, u32[]{:S(2)}, u32[]{:S(2)}) async-start(bf16[8,512,256]{1,2,0:T(8,128)(2,1)} %fusion.16), calls=%async_computation.1 | async-start | bytes 4194304 | tf_op jit(solution)/shard_map/all_to_all | solution.py:47
Sparse Core Ops, SparseCore 0:
  9.8 55.2 all-gather.2
where the time goes:
time: 293 us; the launch traced here: 292 us
  waiting for transfers between devices  155 us (53%)
  other arithmetic  58.2 us (20%)
  blocking collectives  37 us (13%)
  between operations  14.1 us (5%)
  local copies, waits for them, and re-layouts  9.6 us (3%)
  matrix products  9.6 us (3%)
  starting transfers between devices  8.86 us (3%)
    all_gather x1, waiting for transfers between devices, shards(): whole = lax.all_gather(rows, 'dp', axis=0, tiled=True)  57.2 us
    all_to_all x1, waiting for transfers between devices, shards(): held = lax.all_to_all(gram.astype(jnp.bfloat16), 'member', 0, 0)  48.6 us
    all_to_all x1, waiting for transfers between devices, shards(): mixed = lax.all_to_all(mixed, 'member', 0, 0)  48.4 us
    unnamed x7, other arithmetic  43.5 us
    psum x1, blocking collectives, shards(): sums = lax.psum(jnp.stack(sums, axis=1), ('member', 'dp'))  37 us
    another operation x1, other arithmetic, shards(): jnp.stack([sum((mix[m, q] * held[q] for q in range(members))) for m in ra...  6.23 us
  transfers between devices with their start and end apart: 3, of which 3 were waited for; matrix products, arithmetic and copies ran while one was open for 0% of the time, Pallas kernels for 0%

commit v1 on v0

--- a/solution.py
+++ b/solution.py
@@ -39,7 +39,9 @@
     sums = []
     for o in range(pairs + 1):
         sums.append(jnp.sum(held * jnp.roll(held, -o, axis=0), axis=(1, 2)))
-    sums = lax.psum(jnp.stack(sums, axis=1), ("member", "dp"))
+    x = jnp.stack(sums, axis=1)
+    parts = lax.all_gather(x, ("member", "dp"), axis=0, tiled=False)
+    sums = parts.sum(axis=0)
     cka, mix = mixing(sums[:, 0], sums[:, 1:], pair_weight)
     mixed = jnp.stack(
         [sum((mix[m, q] * held[q] for q in range(members))) for m in range(members)]

time: 293 us -> 321 us (1.096)
  blocking collectives: 37 us -> 65.6 us
    all_gather x0 -> x1, blocking collectives: none -> 65.6 us  [shards(): parts = lax.all_gather(x, ('member', 'dp'), axis=0, tiled=False)]
    psum x1 -> x0, blocking collectives: 37 us -> none  [shards(): sums = lax.psum(jnp.stack(sums, axis=1), ('member', 'dp'))]
    unnamed x7 -> x8, other arithmetic: 43.5 us -> 43.5 us
where the time goes in v1:
time: 321 us; the launch traced here: 320 us
  waiting for transfers between devices  155 us (48%)
  blocking collectives  65.6 us (20%)
  other arithmetic  58.3 us (18%)
  between operations  14.2 us (4%)
  local copies, waits for them, and re-layouts  9.61 us (3%)
  matrix products  9.6 us (3%)
  starting transfers between devices  8.25 us (3%)
    all_gather x1, blocking collectives, shards(): parts = lax.all_gather(x, ('member', 'dp'), axis=0, tiled=False)  65.6 us
    all_gather x1, waiting for transfers between devices, shards(): whole = lax.all_gather(rows, 'dp', axis=0, tiled=True)  57.2 us
    all_to_all x1, waiting for transfers between devices, shards(): held = lax.all_to_all(gram.astype(jnp.bfloat16), 'member', 0, 0)  48.6 us
    all_to_all x1, waiting for transfers between devices, shards(): mixed = lax.all_to_all(mixed, 'member', 0, 0)  48.3 us
    unnamed x8, other arithmetic  43.5 us
  transfers between devices with their start and end apart: 3, of which 3 were waited for; matrix products, arithmetic and copies ran while one was open for 0% of the time, Pallas kernels for 0%

profile of v1, /device:TPU:0, one launch (start us, length us, event | category | flops | bytes accessed | tf_op | source)
XLA Modules:
  0.0 320.3 jit_solution(15895080958092633944)
XLA Ops:
  7.2 0.0 all-gather.5.cloned.1.call-start
  7.2 0.7 all-gather.5.cloned.1.call-update
  7.9 57.2 %all-gather.5.cloned.1.call-done = bf16[1,2048,1024]{2,1,0:T(8,128)(2,1)} async-done(((bf16[1,512,1024]{2,1,0:T(8,128)(2,1)}), bf16[1,2048,1024]{2,1,0:T(8,128)(2,1)}) %all-gather.5.cloned.1.call-update) | async-done | bytes 4194320 | tf_op jit(solution)/shard_map/all_gather | solution.py:30
  65.1 0.0 copy-start.1
  65.1 3.0 convert_reduce_fusion
  68.2 0.4 copy-done.1
  68.6 1.3 fusion.1
  69.9 0.0 copy-start
  69.9 1.9 copy-done
  71.8 0.0 copy-done.2
  71.8 3.8 %convert_bitcast_fusion.1 = bf16[8,512,256]{1,2,0:T(8,128)(2,1)} fusion(bf16[8,256,1024]{2,1,0:T(8,128)(2,1)S(1)} %bitcast.138, bf16[1,512,1024]{2,1,0:T(8,128)(2,1)S(1)} %copy-done.2, f32[1024]{0:T(1024)S(1)} %broadcast_multiply_fusion), kind=kOutput, calls=%fused_computation.13 | convolution fusion | flops 2150105088 | bytes 7344128 | tf_op jit(solution)/shard_map/rf,mcf->mrc/dot_general | solution.py:36
  75.5 4.6 %all-to-all-start = ((bf16[8,512,256]{1,2,0:T(8,128)(2,1)}), bf16[8,512,256]{1,2,0:T(8,128)(2,1)S(1)}, u32[]{:S(2)}, u32[]{:S(2)}) async-start(bf16[8,512,256]{1,2,0:T(8,128)(2,1)} %convert_bitcast_fusion.1), calls=%async_computation | async-start | bytes 4194304 | tf_op jit(solution)/shard_map/all_to_all | solution.py:37
  80.1 0.1 slice.447
  80.2 0.1 slice.450
  80.3 0.1 slice.453
  80.4 0.1 copy.21
  80.4 0.1 copy.22
  80.5 0.1 copy.12
  80.6 48.6 %all-to-all-done = bf16[8,512,256]{1,2,0:T(8,128)(2,1)S(1)} async-done(((bf16[8,512,256]{1,2,0:T(8,128)(2,1)}), bf16[8,512,256]{1,2,0:T(8,128)(2,1)S(1)}, u32[]{:S(2)}, u32[]{:S(2)}) %all-to-all-start) | async-done | bytes 2097184 | tf_op jit(solution)/shard_map/all_to_all | solution.py:37
  129.2 0.5 slice.526
  129.7 0.4 slice.528
  130.1 0.4 slice.530
  130.5 0.2 slice.531
  130.7 0.1 slice.529
  130.8 0.1 slice.527
  130.9 0.0 copy-start.3
  130.9 1.8 multiply_reduce_fusion
  132.7 65.6 %all-gather.2 = f32[32,8,4]{1,2,0:T(4,128)S(1)} all-gather(f32[1,8,4]{1,2,0:T(4,128)S(1)} %maximum_bitcast_fusion), channel_id=3, replica_groups=mesh['member'=8,'dp'=4] {'member','dp'}, dimensions={0}, use_global_device_ids=true | all-gather | bytes 4224 | tf_op jit(solution)/shard_map/all_gather | solution.py:43
  198.4 0.5 slice.430
  198.9 0.1 slice_bitcast_fusion.7
  199.0 0.1 slice_bitcast_fusion.6
  199.1 0.1 slice_bitcast_fusion.4
  199.1 0.7 maximum_bitcast_fusion.1
  199.9 0.1 maximum_bitcast_fusion.2
  199.9 0.1 maximum_bitcast_fusion.3
  200.0 0.0 copy-done.3
  200.0 0.6 slice.440
  200.6 0.1 slice.442
  200.7 0.1 slice.444
  200.8 0.7 slice_bitcast_fusion.1
  201.5 0.1 copy.15
  201.6 0.1 fusion.18
  201.7 0.1 copy.16
  201.8 0.1 maximum_multiply_fusion.5
  201.8 0.1 copy.17
  201.9 0.1 bitcast_add_fusion
  202.0 0.7 fusion.26
  202.7 0.6 fusion.27
  203.3 0.7 fusion.25
  204.0 0.7 fusion.24
  204.8 0.6 convert_element_type.47
  205.3 6.4 %fusion.9 = bf16[8,512,256]{1,2,0:T(8,128)(2,1)} fusion(f32[8,512,256]{1,2,0:T(8,128)S(1)} %convert_element_type.47, f32[]{:T(128)} %bitcast.35, f32[]{:T(128)} %bitcast.34, f32[]{:T(128)} %bitcast.33, f32[]{:T(128)} %bitcast.32, f32[]{:T(128)} %bitcast.31, f32[]{:T(128)} %bitcast.30, f32[]{:T(128)} %bitcast.29, f32[]{:T(128)} %bitcast.28), kind=kLoop, calls=%fused_computation.25 | loop fusion | flops 2097151 | bytes 4456480
  211.7 6.1 %fusion.10 = bf16[8,512,256]{1,2,0:T(8,128)(2,1)} fusion(bf16[8,512,256]{1,2,0:T(8,128)(2,1)} %fusion.9, f32[8,512,256]{1,2,0:T(8,128)S(1)} %convert_element_type.47, f32[]{:T(128)} %bitcast.43, f32[]{:T(128)} %bitcast.42, f32[]{:T(128)} %bitcast.41, f32[]{:T(128)} %bitcast.40, f32[]{:T(128)} %bitcast.39, f32[]{:T(128)} %bitcast.38, f32[]{:T(128)} %bitcast.37, ...), kind=kLoop, calls=%fused_computation.26 | loop fusion | flops 2097152 | bytes 4460544
  217.8 6.1 %fusion.11 = bf16[8,512,256]{1,2,0:T(8,128)(2,1)} fusion(bf16[8,512,256]{1,2,0:T(8,128)(2,1)} %fusion.10, f32[8,512,256]{1,2,0:T(8,128)S(1)} %convert_element_type.47, f32[]{:T(128)} %bitcast.51, f32[]{:T(128)} %bitcast.50, f32[]{:T(128)} %bitcast.49, f32[]{:T(128)} %bitcast.48, f32[]{:T(128)} %bitcast.47, f32[]{:T(128)} %bitcast.46, f32[]{:T(128)} %bitcast.45, ...), kind=kLoop, calls=%fused_computation.27 | loop fusion | flops 2097152 | bytes 4460544
  224.0 6.1 %fusion.12 = bf16[8,512,256]{1,2,0:T(8,128)(2,1)} fusion(bf16[8,512,256]{1,2,0:T(8,128)(2,1)} %fusion.11, f32[8,512,256]{1,2,0:T(8,128)S(1)} %convert_element_type.47, f32[]{:T(128)} %bitcast.59, f32[]{:T(128)} %bitcast.58, f32[]{:T(128)} %bitcast.57, f32[]{:T(128)} %bitcast.56, f32[]{:T(128)} %bitcast.55, f32[]{:T(128)} %bitcast.54, f32[]{:T(128)} %bitcast.53, ...), kind=kLoop, calls=%fused_computation.28 | loop fusion | flops 2097152 | bytes 4460544
  230.0 6.3 %fusion.13 = bf16[8,512,256]{1,2,0:T(8,128)(2,1)} fusion(bf16[8,512,256]{1,2,0:T(8,128)(2,1)} %fusion.12, f32[8,512,256]{1,2,0:T(8,128)S(1)} %convert_element_type.47, f32[]{:T(128)} %bitcast.67, f32[]{:T(128)} %bitcast.66, f32[]{:T(128)} %bitcast.65, f32[]{:T(128)} %bitcast.64, f32[]{:T(128)} %bitcast.63, f32[]{:T(128)} %bitcast.62, f32[]{:T(128)} %bitcast.61, ...), kind=kLoop, calls=%fused_computation.29 | loop fusion | flops 2097152 | bytes 4460544
  236.4 6.2 %fusion.14 = bf16[8,512,256]{1,2,0:T(8,128)(2,1)} fusion(bf16[8,512,256]{1,2,0:T(8,128)(2,1)} %fusion.13, f32[8,512,256]{1,2,0:T(8,128)S(1)} %convert_element_type.47, f32[]{:T(128)} %bitcast.75, f32[]{:T(128)} %bitcast.74, f32[]{:T(128)} %bitcast.73, f32[]{:T(128)} %bitcast.72, f32[]{:T(128)} %bitcast.71, f32[]{:T(128)} %bitcast.70, f32[]{:T(128)} %bitcast.69, ...), kind=kLoop, calls=%fused_computation.30 | loop fusion | flops 2097152 | bytes 4460544
  242.6 6.2 %fusion.15 = bf16[8,512,256]{1,2,0:T(8,128)(2,1)} fusion(bf16[8,512,256]{1,2,0:T(8,128)(2,1)} %fusion.14, f32[8,512,256]{1,2,0:T(8,128)S(1)} %convert_element_type.47, f32[]{:T(128)} %bitcast.83, f32[]{:T(128)} %bitcast.82, f32[]{:T(128)} %bitcast.81, f32[]{:T(128)} %bitcast.80, f32[]{:T(128)} %bitcast.79, f32[]{:T(128)} %bitcast.78, f32[]{:T(128)} %bitcast.77, ...), kind=kLoop, calls=%fused_computation.31 | loop fusion | flops 2097152 | bytes 4460544
  248.8 6.2 %fusion.16 = bf16[8,512,256]{1,2,0:T(8,128)(2,1)} fusion(bf16[8,512,256]{1,2,0:T(8,128)(2,1)} %fusion.15, f32[8,512,256]{1,2,0:T(8,128)S(1)} %convert_element_type.47, f32[]{:T(128)} %bitcast.91, f32[]{:T(128)} %bitcast.90, f32[]{:T(128)} %bitcast.89, f32[]{:T(128)} %bitcast.88, f32[]{:T(128)} %bitcast.87, f32[]{:T(128)} %bitcast.86, f32[]{:T(128)} %bitcast.85, ...), kind=kLoop, calls=%fused_computation.32 | loop fusion | flops 2097152 | bytes 4460544 | tf_op jit(solution)/shard_map/stack | solution.py:46
  255.0 3.6 %all-to-all-start.1 = ((bf16[8,512,256]{1,2,0:T(8,128)(2,1)}), bf16[8,512,256]{1,2,0:T(8,128)(2,1)S(1)}, u32[]{:S(2)}, u32[]{:S(2)}) async-start(bf16[8,512,256]{1,2,0:T(8,128)(2,1)} %fusion.16), calls=%async_computation.1 | async-start | bytes 4194304 | tf_op jit(solution)/shard_map/all_to_all | solution.py:49
  258.7 0.1 constant_dynamic-slice_fusion
  258.7 0.6 copy.19
  259.3 48.3 %all-to-all-done.1 = bf16[8,512,256]{1,2,0:T(8,128)(2,1)S(1)} async-done(((bf16[8,512,256]{1,2,0:T(8,128)(2,1)}), bf16[8,512,256]{1,2,0:T(8,128)(2,1)S(1)}, u32[]{:S(2)}, u32[]{:S(2)}) %all-to-all-start.1) | async-done | bytes 2097184 | tf_op jit(solution)/shard_map/all_to_all | solution.py:49
  307.6 5.9 %fusion.5 = f32[1,512,1024]{2,1,0:T(8,128)} fusion(bf16[8,512,256]{1,2,0:T(8,128)(2,1)S(1)} %all-to-all-done.1, bf16[8,256,1024]{2,1,0:T(8,128)(2,1)} %bitcast.139), kind=kOutput, calls=%fused_computation.12 | convolution fusion | flops 2148007936 | bytes 8388608 | tf_op jit(solution)/shard_map/jrc,jcf->rf/dot_general | solution.py:50
  (14 shorter events, 0.1 us)
Async XLA Ops:
  7.2 58.0 %all-gather.5.cloned.1.call-start = ((), (), s32[]{:S(2)}) async-start(), calls=%async_computation.2 | async-start | bytes 5242880 | tf_op jit(solution)/shard_map/all_gather | solution.py:30
  65.1 3.4 %copy-start.1 = (bf16[1,2048,1024]{2,1,0:T(8,128)(2,1)S(1)}, bf16[1,2048,1024]{2,1,0:T(8,128)(2,1)}, u32[]{:S(2)}) copy-start(bf16[1,2048,1024]{2,1,0:T(8,128)(2,1)} %all-gather.5.cloned.1.call-done) | copy-start | bytes 12582916
  68.6 3.2 copy-start.2
  69.9 1.9 copy-start
  75.5 53.6 %all-to-all-start = ((bf16[8,512,256]{1,2,0:T(8,128)(2,1)}), bf16[8,512,256]{1,2,0:T(8,128)(2,1)S(1)}, u32[]{:S(2)}, u32[]{:S(2)}) async-start(bf16[8,512,256]{1,2,0:T(8,128)(2,1)} %convert_bitcast_fusion.1), calls=%async_computation | async-start | bytes 4194304 | tf_op jit(solution)/shard_map/all_to_all | solution.py:37
  130.9 69.1 %copy-start.3 = (f32[8,3]{0,1:T(4,128)S(1)}, f32[8,3]{0,1:T(4,128)}, u32[]{:S(2)}) copy-start(f32[8,3]{0,1:T(4,128)} %param.3) | copy-start | bytes 292
  255.0 52.6 %all-to-all-start.1 = ((bf16[8,512,256]{1,2,0:T(8,128)(2,1)}), bf16[8,512,256]{1,2,0:T(8,128)(2,1)S(1)}, u32[]{:S(2)}, u32[]{:S(2)}) async-start(bf16[8,512,256]{1,2,0:T(8,128)(2,1)} %fusion.16), calls=%async_computation.1 | async-start | bytes 4194304 | tf_op jit(solution)/shard_map/all_to_all | solution.py:49
Sparse Core Ops, SparseCore 0:
  9.8 55.2 all-gather.4
